TPU v7x, 32 devices: a whole 2x2x4 slice. The times are simulated.
32 devices in a mesh: dp: 4 (over x, core), tm: 8 (over z, y).
Axes of the slice: x: 2, y: 2, z: 4, core: 2. Of those that a mesh axis runs over, the one named last changes fastest.
Arguments:
- latent: float32 [4, 64, 4096], P('dp', None, 'tm'), may hold values from -40 to 40
- target: float32 [4, 8192], P('dp', 'tm'), may hold values from -20 to 20
- up_kernel: float32 [4, 32, 64], replicated, may hold values from -0.5 to 0.5
- inner_kernel: float32 [3, 16, 32], replicated, may hold values from -0.625 to 0.625
- outer_kernel: float32 [32, 16], replicated, may hold values from -1.5 to 1.5
- out_kernel: float32 [7, 32], replicated, may hold values from -0.375 to 0.375
Outputs:
- latent_grad: float32 [4, 64, 4096], P('dp', None, 'tm')
- up_update: float32 [4, 32, 64], replicated
- inner_update: float32 [3, 16, 32], replicated
- outer_update: float32 [32, 16], replicated
- out_update: float32 [7, 32], replicated
All inputs are finite; a program needn't handle non-finite values.
Results may differ from a plain program's by a relative error of at most 0.0003.
Values sent between devices are 32-bit elements; how exact they have to be, the bound alone decides.
No kernel may reach another device: no remote copies, remote signals or barrier semaphores. Data moves between devices by JAX's collectives and lax.ppermute only.
A program may use at most 64 MiB of HBM per device.

v0:
```python
import jax
import jax.numpy as jnp
from jax import lax
from jax.sharding import PartitionSpec as P

MELS = 64
WIN_COARSE = 1024
WIN_FINE = 256
LOSS_WEIGHTS = (0.25, 0.5, 0.5)


def padded_2(cells, sides, width):
    for axis, dim in sides:
        count = lax.axis_size(axis)
        ends = count - 1
        head = lax.slice_in_dim(cells, 0, width, axis=dim)
        tail = lax.slice_in_dim(cells, cells.shape[dim] - width, cells.shape[dim], axis=dim)
        cells = jnp.concatenate(
            [
                lax.ppermute(tail, axis, [(i, (i + 1) % count) for i in range(ends)]),
                cells,
                lax.ppermute(head, axis, [((i + 1) % count, i) for i in range(ends)]),
            ],
            axis=dim,
        )
    return cells


def from_behind(x, axis, by):
    peers = lax.axis_size(axis)
    pairs = [(i, i + by) for i in range(peers) if 0 <= i + by < peers]
    return lax.ppermute(x, axis, pairs)


def product(form, left, right):
    return jnp.einsum(
        form, left, right, precision=lax.Precision.HIGHEST, preferred_element_type=jnp.float32
    )


def mel_bank(window, mel_count):
    half_window = window // 2
    top_mel = 2595.0 * jnp.log10(1.0 + 12000.0 / 700.0)
    points = (jnp.arange(mel_count + 1, dtype=jnp.float32) + 1.0) / (mel_count + 2.0) * top_mel
    centers = 700.0 * (jnp.power(10.0, points / 2595.0) - 1.0) / 12000.0 * half_window
    spacing = jnp.maximum(centers[1:] - centers[:-1], 1.0)
    places = jnp.arange(half_window, dtype=jnp.float32)[:, None]
    return jnp.maximum(0.0, 1.0 - jnp.abs(places - centers[None, :mel_count]) / spacing[None, :])


def dft_table(window):
    half_window = window // 2
    sample = jnp.arange(window, dtype=jnp.int32)[:, None]
    freq_index = jnp.arange(half_window, dtype=jnp.int32)[None, :]
    angles = (sample * freq_index % window).astype(jnp.float32) * (2.0 * jnp.pi / window)
    hann_taper = 0.5 - 0.5 * jnp.cos(sample.astype(jnp.float32) * (2.0 * jnp.pi / window))
    return jnp.concatenate([hann_taper * jnp.cos(angles), -hann_taper * jnp.sin(angles)], axis=1)


def framed(signal, window, frame_count):
    hop_size = window // 4
    blocks = signal.reshape(signal.shape[:-1] + (frame_count + 3, hop_size))
    return jnp.concatenate(
        [blocks[..., offset : offset + frame_count, :] for offset in range(4)], axis=-1
    )


def mel_energy(signal, window, frame_count):
    frames = framed(signal, window, frame_count)
    spectra = product("...nf,fk->...nk", frames, dft_table(window))
    half_window = window // 2
    energy = spectra[..., :half_window] ** 2 + spectra[..., half_window:] ** 2
    return product("...nk,km->...nm", energy, mel_bank(window, MELS))


def spectral_loss(signal, target_mel, window, frame_count):
    level = jnp.sqrt(mel_energy(signal, window, frame_count) + 1.0)
    return jnp.sum((level - jnp.sqrt(target_mel + 1.0)) ** 2)


def elu_slope(values):
    return jnp.where(values > 0, 1.0, jnp.exp(jnp.minimum(values, 0.0)))


def apply_mask(values, mask):
    return values * mask


def upsample_forward(values, kernel, stride, previous):
    lagged = jnp.concatenate([previous, values[:, :, :-1]], axis=2)
    phases = product("pij,bjm->bimp", kernel[:stride], values) + product(
        "pij,bjm->bimp", kernel[stride:], lagged
    )
    return (phases.reshape(phases.shape[0], phases.shape[1], -1), lagged)


def taps_forward(padded, kernel, length):
    summed = product("oi,bil->bol", kernel[0], padded[:, :, :length])
    for offset in range(1, kernel.shape[0]):
        summed = summed + product(
            "oi,bil->bol", kernel[offset], padded[:, :, offset : offset + length]
        )
    return summed


def decode_forward(activated, weights, movers, clip_mask):
    up_kernel, inner_kernel, outer_kernel, out_kernel = weights
    lend_frame, border_inner, border_output = movers
    upper, lagged = upsample_forward(activated, up_kernel, 2, lend_frame(activated[:, :, -1:]))
    upper = apply_mask(upper, clip_mask)
    padded_inner = border_inner(jax.nn.elu(upper))
    inner_out = taps_forward(padded_inner, inner_kernel, upper.shape[2])
    hidden = jax.nn.elu(inner_out)
    mixed = apply_mask(upper + product("oi,bil->bol", outer_kernel, hidden), clip_mask)
    padded_output = border_output(jax.nn.elu(mixed))
    waveform = taps_forward(padded_output, out_kernel[:, None, :], upper.shape[2])[:, 0, :]
    return (waveform, (upper, lagged, padded_inner, inner_out, hidden, mixed, padded_output))


def taps_backward(grad_out, padded, kernel, length, keep):
    tap_count = kernel.shape[0]
    row_grad = apply_mask(grad_out, keep)
    kernel_rows = jnp.stack(
        [
            product("nbol,bil->nboi", row_grad, padded[:, :, offset : offset + length])
            for offset in range(tap_count)
        ],
        axis=2,
    )
    spread = jnp.zeros(grad_out.shape[:2] + (kernel.shape[2], length + tap_count - 1), jnp.float32)
    for offset in range(tap_count):
        moved = product("oi,nbol->nbil", kernel[offset], grad_out)
        spread = spread + jnp.pad(moved, ((0, 0), (0, 0), (0, 0), (offset, tap_count - 1 - offset)))
    return (kernel_rows, spread)


def rims_backward(spread, rim_width):
    interior = spread[..., rim_width:-rim_width]
    return interior


def residual_backward(
    grad_mixed, upper, padded, inner_out, hidden, inner_kernel, outer_kernel, keep
):
    length = upper.shape[-1]
    outer_rows = product("nbol,bil->nboi", apply_mask(grad_mixed, keep), hidden)
    grad_inner = product("oi,nbol->nbil", outer_kernel, grad_mixed) * elu_slope(inner_out)
    inner_rows, spread = taps_backward(grad_inner, padded, inner_kernel, length, keep)
    grad_rectified = rims_backward(spread, 1)
    return (grad_mixed + grad_rectified * elu_slope(upper), inner_rows, outer_rows)


def upsample_backward(grad_upper, values, lagged, kernel, stride, keep):
    phase_shape = grad_upper.shape[:3] + (values.shape[-1], stride)
    grad_phase = grad_upper.reshape(phase_shape)
    row_phase = apply_mask(grad_upper, keep).reshape(phase_shape)
    first_rows = product("nbimp,bjm->nbpij", row_phase, values)
    second_rows = product("nbimp,bjm->nbpij", row_phase, lagged)
    grad_values = product("pij,nbimp->nbjm", kernel[:stride], grad_phase)
    grad_lagged = product("pij,nbimp->nbjm", kernel[stride:], grad_phase)
    arrived = jnp.zeros_like(grad_lagged[..., :1])
    grad_values = grad_values + jnp.concatenate([grad_lagged[..., 1:], arrived], axis=-1)
    return (grad_values, jnp.concatenate([first_rows, second_rows], axis=2))


def local(latent, target, up_kernel, inner_kernel, outer_kernel, out_kernel):
    weights = (up_kernel, inner_kernel, outer_kernel, out_kernel)
    clips_here = target.shape[0]
    samples = target.shape[1]
    frames_here = latent.shape[2]
    latent_in = padded_2(latent, (("tm", 2),), 4)
    start_frame = 4
    margin = 8

    def lend_frame(edge):
        return jnp.zeros_like(edge)

    def border_inner(values):
        return jnp.pad(values, ((0, 0), (0, 0), (1, 1)))

    def border_output(values):
        return jnp.pad(values, ((0, 0), (0, 0), (3, 3)))

    shard_index = lax.axis_index("tm")
    shard_total = lax.axis_size("tm")
    wide_length = samples + 2 * margin
    local_places = jnp.arange(wide_length, dtype=jnp.int32)
    clip_places = samples * shard_index - margin + local_places
    clip_mask = ((clip_places >= 0) & (clip_places < samples * shard_total)).astype(jnp.float32)
    keep_rows = ((local_places >= margin) & (local_places < margin + samples)).astype(jnp.float32)
    activated = jax.nn.elu(latent_in)
    wave_all, saved = decode_forward(
        activated, weights, (lend_frame, border_inner, border_output), clip_mask
    )
    upper, lagged, padded_inner, inner_out, hidden, mixed, padded_output = saved
    waveform = wave_all[:, margin : margin + samples]
    tail_length = 3 * WIN_COARSE // 4
    wave_next, target_next = from_behind(
        (waveform[:, :tail_length], target[:, :tail_length]), "tm", -1
    )
    long_wave = jnp.concatenate([waveform, wave_next], axis=1)
    long_target = jnp.concatenate([target, target_next], axis=1)
    gradients = [2.0 * (waveform - target)]
    tails = []
    for window in (WIN_COARSE, WIN_FINE):
        hop_size = window // 4
        frame_count = samples // hop_size
        span = samples + 3 * hop_size
        target_mel = mel_energy(long_target[:, :span], window, frame_count)

        def scale_loss(signal):
            return spectral_loss(signal, target_mel, window, frame_count)

        local_grad = jax.grad(scale_loss)(long_wave[:, :span])
        gradients.append(local_grad[:, :samples])
        tails.append(jnp.pad(local_grad[:, samples:], ((0, 0), (0, tail_length - 3 * hop_size))))
    coarse_in, fine_in = from_behind((tails[0], tails[1]), "tm", 1)
    gradients[1] = gradients[1] + jnp.pad(coarse_in, ((0, 0), (0, samples - tail_length)))
    gradients[2] = gradients[2] + jnp.pad(fine_in, ((0, 0), (0, samples - tail_length)))
    squares = jnp.stack([jnp.sum(member * member, axis=1) for member in gradients], axis=1)
    squares = lax.psum(squares, "tm")
    total_samples = samples * lax.axis_size("tm")
    grad_scale = jnp.asarray(LOSS_WEIGHTS, jnp.float32)[None, :] / jnp.sqrt(
        squares / total_samples + 1e-06
    )
    streams = (
        gradients[0] * grad_scale[:, 0, None]
        + gradients[1] * grad_scale[:, 1, None]
        + gradients[2] * grad_scale[:, 2, None]
    )[None]
    row_weights = jnp.ones((1, clips_here), jnp.float32)
    streams_wide = padded_2(streams, (("tm", 2),), 8)
    wave_length = mixed.shape[2]
    out_taps = out_kernel[:, None, :]
    kernel_rows_out, spread_out = taps_backward(
        streams_wide[:, :, None, :], padded_output, out_taps, wave_length, keep_rows
    )
    out_rows = kernel_rows_out[:, :, :, 0, :]
    grad_final = rims_backward(spread_out, 3)
    grad_mixed = apply_mask(grad_final * elu_slope(mixed), clip_mask)
    grad_upper, inner_rows, outer_rows = residual_backward(
        grad_mixed, upper, padded_inner, inner_out, hidden, inner_kernel, outer_kernel, keep_rows
    )
    grad_activated, up_rows = upsample_backward(
        apply_mask(grad_upper, clip_mask), activated, lagged, up_kernel, 2, keep_rows
    )
    grad_latent_rows = grad_activated[..., start_frame : start_frame + frames_here] * elu_slope(
        latent
    )
    latent_grad = product("nb,nbcm->bcm", row_weights, grad_latent_rows)
    local_totals = [
        product("nb,nb...->...", row_weights, member)
        for member in (up_rows, inner_rows, outer_rows, out_rows)
    ]
    param_count = sum((member.size for member in local_totals))
    summed = lax.psum(
        (local_totals[0], local_totals[1], local_totals[2], local_totals[3]), ("dp", "tm")
    )
    squares_all = sum((jnp.sum(member * member) for member in summed))
    factor = jnp.minimum(1.0, 1.0 / jnp.sqrt(squares_all / param_count + 1e-06))
    updates = [member * factor for member in summed]
    return (latent_grad, updates[0], updates[1], updates[2], updates[3])


def solution(mesh):
    placed = (P("dp", None, "tm"), P("dp", "tm"), P(), P(), P(), P())
    return jax.shard_map(
        local,
        mesh=mesh,
        in_specs=placed,
        out_specs=(P("dp", None, "tm"), P(), P(), P(), P()),
        check_vma=False,
    )
```

profile of v0, /device:TPU:0, one launch (start us, length us, event | category | flops | bytes accessed | tf_op | source)
XLA Modules:
  0.0 188.2 jit_solution(7671481007626582187)
XLA Ops:
  0.6 1.3 slice.296
  1.9 1.3 collective-permute-start.3
  4.1 5.5 %collective-permute-start = (f32[1,64,4]{2,1,0:T(8,128)S(1)}, f32[1,64,4]{2,1,0:T(8,128)S(1)}, u32[]{:S(2)}, u32[]{:S(2)}) collective-permute-start(f32[1,64,4]{2,1,0:T(8,128)S(1)} %get-tuple-element.15), channel_id=1, source_target_pairs={{0,1},{1,2},{2,3},{3,4},{4,5},{5,6},{6,7},{8,9},{9,10},{10,11},{11... | collective-permute-start | bytes 3080 | tf_op jit(solution)/shard_map/ppermute | solution.py:20
  9.6 1.3 collective-permute-start.1
  12.3 1.6 slice_bitcast_fusion.6
  13.9 1.2 sine_multiply_fusion.1
  15.1 9.4 %sine_multiply_fusion = (f32[1024,512]{1,0:T(8,128)S(1)}, f32[1024,512]{1,0:T(8,128)}) fusion(f32[1024]{0:T(1024)S(1)} %fusion.218, f32[1024]{0:T(1024)S(1)} %multiply_subtract_fusion), kind=kLoop, calls=%fused_computation.21 | loop fusion | flops 8388608 | bytes 4202496 | tf_op jit(solution)/shard_map/jvp()/mul | solution.py:57
  25.3 1.1 compare_select_fusion
  26.7 1.2 copy.16
  28.1 1.0 fusion.69
  29.1 1.3 convolution_add_fusion.1
  30.4 1.0 fusion.5
  31.4 1.3 compare_select_fusion.9
  32.7 1.0 convolution_reduce_fusion.2
  33.7 1.0 convolution_reduce_fusion.1
  34.7 1.0 convolution_reduce_fusion
  35.7 1.0 convolution_reduce_fusion.5
  36.7 1.0 convolution_reduce_fusion.4
  37.6 1.0 convolution_reduce_fusion.6
  38.6 1.0 convolution_reduce_fusion.3
  39.6 2.0 %multiply_reduce_fusion.6 = (f32[]{:T(128)}, f32[1,1024]{1,0:T(1,128)}, f32[1,1792]{1,0:T(1,128)S(1)}) fusion(f32[1,1024]{1,0:T(1,128)} %param.8, f32[1,1040]{1,0:T(1,128)S(1)} %squeeze.11), kind=kLoop, calls=%fused_computation.340 | loop fusion | flops 4094 | bytes 16388 | tf_op jit(solution)/shard_map/reduce_sum | solution.py:220
  42.3 1.3 collective-permute-start.2
  45.4 1.3 reduce.11
  46.7 1.3 reshape.962
  48.0 1.4 reshape.970
  51.1 4.3 %fusion.15 = f32[1,4,1024]{2,1,0:T(4,128)} fusion(f32[1024,512]{1,0:T(8,128)S(1)} %get-tuple-element.77, f32[1024,512]{1,0:T(8,128)} %get-tuple-element.78, f32[1,4,256]{2,1,0:T(4,128)S(1)} %get-tuple-element.45, f32[1,4,256]{2,1,0:T(4,128)S(1)} %get-tuple-element.46, f32[1,4,256]{2,1,0:T(4,128)S(1)} %get-tuple-element.47, ...), kind=kOutput, calls=%fused_computation.33 | convolution fusion | flops 51392512 | bytes 4227072 | tf_op jit(solution)/shard_map/...nf,fk->...nk/dot_general | solution.py:36
  55.4 0.9 convolution_bitcast_fusion.10
  56.3 1.3 maximum_reduce_fusion
  57.6 1.3 reshape.959
  58.9 1.3 fusion.210
  60.2 1.4 reshape.967
  61.6 1.4 fusion.285
  63.0 0.9 fusion.283
  63.9 1.2 convolution_bitcast_fusion.11
  65.9 0.9 fusion.20
  67.6 1.3 convolution_bitcast_fusion.9
  69.7 1.4 reshape.974
  71.7 6.2 %collective-permute-start.5 = (f32[1,768]{1,0:T(1,128)S(1)}, f32[1,768]{1,0:T(1,128)S(1)}, u32[]{:S(2)}, u32[]{:S(2)}) collective-permute-start(f32[1,768]{1,0:T(1,128)S(1)} %pad.112), channel_id=1, source_target_pairs={{0,1},{1,2},{2,3},{3,4},{4,5},{5,6},{6,7},{8,9},{9,10},{10,11},{11... | collective-permute-start | bytes 9224 | tf_op jit(solution)/shard_map/ppermute | solution.py:32
  78.0 3.7 %fusion.14 = f32[1,4,1024]{2,1,0:T(4,128)S(1)} fusion(f32[1024,512]{1,0:T(8,128)S(1)} %get-tuple-element.77, f32[1024,512]{1,0:T(8,128)} %get-tuple-element.78, f32[1,4,256]{2,1,0:T(4,128)} %get-tuple-element.49, f32[1,4,256]{2,1,0:T(4,128)} %get-tuple-element.50, f32[1,4,256]{2,1,0:T(4,128)} %get-tuple-element.51, f32[1,4,256]{2,1,0:T(4,128)} %get-tuple-element.48), kind=kOutput, calls=%fused_computation.32 | convolution fusion | flops 51392512 | bytes 4227072 | tf_op jit(solution)/shard_map/jvp(...nf,fk->...nk)/dot_general | solution.py:36
  83.3 3.5 %fusion.16 = f32[1,4,1024]{2,1,0:T(4,128)S(1)} fusion(f32[1024,512]{1,0:T(8,128)S(1)} %get-tuple-element.77, f32[1024,512]{1,0:T(8,128)S(1)} %copy-done.1, f32[1,4,512]{2,1,0:T(4,128)S(1)} %get-tuple-element.18, f32[1,4,512]{2,1,0:T(4,128)S(1)} %get-tuple-element.17), kind=kOutput, calls=%fused_computation.34 | convolution fusion | flops 51384320 | bytes 4227072 | tf_op jit(solution)/shard_map/transpose(jvp(...nf,fk->...nk))/dot_general | solution.py:36
  86.9 5.0 %collective-permute-start.4 = (f32[1,768]{1,0:T(1,128)S(1)}, f32[1,768]{1,0:T(1,128)S(1)}, u32[]{:S(2)}, u32[]{:S(2)}) collective-permute-start(f32[1,768]{1,0:T(1,128)S(1)} %slice.347), channel_id=1, source_target_pairs={{0,1},{1,2},{2,3},{3,4},{4,5},{5,6},{6,7},{8,9},{9,10},{10,11},{11... | collective-permute-start | bytes 9224 | tf_op jit(solution)/shard_map/ppermute | solution.py:32
  93.8 2.0 %pad_maximum_fusion.16 = f32[1,3]{1,0:T(1,128)S(1)} fusion(f32[1,1]{1,0:T(1,128)} %bitcast.63, f32[1,1]{1,0:T(1,128)} %bitcast.53, f32[1,1]{1,0:T(1,128)} %bitcast.43), kind=kLoop, calls=%fused_computation.344 | loop fusion | flops 6 | bytes 24 | tf_op jit(solution)/shard_map/stack | solution.py:220
  96.0 22.0 %psum.35 = f32[1,3]{1,0:T(1,128)S(1)} all-reduce(f32[1,3]{1,0:T(1,128)S(1)} %pad_maximum_fusion.16), channel_id=1, replica_groups=mesh['dp'=4,'tm'=8] {'tm'}, use_global_device_ids=true, to_apply=%region_3.4 | all-reduce | flops 3 | bytes 24 | tf_op jit(solution)/shard_map/psum | solution.py:221
  119.8 2.1 %add_bitcast_fusion.1 = f32[1,1,1024]{2,1,0:T(1,128)S(1)} fusion(f32[1,1024]{1,0:T(1,128)S(1)} %get-tuple-element.14, f32[1,1024]{1,0:T(1,128)S(1)} %get-tuple-element.12, f32[]{:T(128)} %bitcast.66, f32[]{:T(128)} %bitcast.65, f32[]{:T(128)} %bitcast.64, f32[1,1024]{1,0:T(1,128)} %param.8, f32[1,1040]{1,0:T(1,128)} %copy-done.14), kind=kLoop, calls=%fused_computation.336 | loop fusion | flops 6144 | bytes 20492 | tf_op jit(solution)/shard_map/broadcast_in_dim | solution.py:226
  122.0 1.3 collective-permute-start.7
  123.3 4.5 %collective-permute-start.6 = (f32[1,1,8]{2,1,0:T(1,128)S(1)}, f32[1,1,8]{2,1,0:T(1,128)S(1)}, u32[]{:S(2)}, u32[]{:S(2)}) collective-permute-start(f32[1,1,8]{2,1,0:T(1,128)S(1)} %get-tuple-element.62), channel_id=1, source_target_pairs={{0,1},{1,2},{2,3},{3,4},{4,5},{5,6},{6,7},{8,9},{9,10},{10,11},{11... | collective-permute-start | bytes 104 | tf_op jit(solution)/shard_map/ppermute | solution.py:20
  127.8 1.3 collective-permute-done.6
  136.8 41.8 %all-reduce.29 = (f32[4,32,64]{2,1,0:T(8,128)S(1)}, f32[3,16,32]{2,1,0:T(8,128)S(1)}, f32[32,16]{0,1:T(8,128)S(1)}, f32[7,32]{1,0:T(8,128)S(1)}) all-reduce(f32[4,32,64]{2,1,0:T(8,128)S(1)} %maximum_bitcast_fusion, f32[3,16,32]{2,1,0:T(8,128)S(1)} %maximum_bitcast_fusion.1, ...), channel_id=1, replica_groups=mesh['dp'=4,'tm'=8] {'dp','tm'}, use_global_device_ids=true, to_apply=%region_4.5 | all-reduce | flops 10464 | bytes 83712 | tf_op jit(solution)/shard_map/psum | solution.py:256
  (141 shorter events, 30.2 us)
Async XLA Ops:
  0.6 30.8 %copy-start = (f32[32,16]{0,1:T(8,128)S(1)}, f32[32,16]{0,1:T(8,128)}, u32[]{:S(2)}) copy-start(f32[32,16]{0,1:T(8,128)} %param.11) | copy-start | bytes 6148
  1.9 41.6 %collective-permute-start.3 = (f32[1,768]{1,0:T(1,128)}, f32[1,768]{1,0:T(1,128)}, u32[]{:S(2)}, u32[]{:S(2)}) collective-permute-start(f32[1,768]{1,0:T(1,128)} %slice.296), channel_id=1, source_target_pairs={{1,0},{2,1},{3,2},{4,3},{5,4},{6,5},{7,6},{9,8},{10,9},{11,10},{12... | collective-permute-start | bytes 9224 | tf_op jit(solution)/shard_map/ppermute | solution.py:32
  4.1 20.5 %collective-permute-start = (f32[1,64,4]{2,1,0:T(8,128)S(1)}, f32[1,64,4]{2,1,0:T(8,128)S(1)}, u32[]{:S(2)}, u32[]{:S(2)}) collective-permute-start(f32[1,64,4]{2,1,0:T(8,128)S(1)} %get-tuple-element.15), channel_id=1, source_target_pairs={{0,1},{1,2},{2,3},{3,4},{4,5},{5,6},{6,7},{8,9},{9,10},{10,11},{11... | collective-permute-start | bytes 3080 | tf_op jit(solution)/shard_map/ppermute | solution.py:20
  9.6 15.0 %collective-permute-start.1 = (f32[1,64,4]{2,1,0:T(8,128)S(1)}, f32[1,64,4]{2,1,0:T(8,128)S(1)}, u32[]{:S(2)}, u32[]{:S(2)}) collective-permute-start(f32[1,64,4]{2,1,0:T(8,128)S(1)} %get-tuple-element.16), channel_id=1, source_target_pairs={{1,0},{2,1},{3,2},{4,3},{5,4},{6,5},{7,6},{9,8},{10,9},{11,10},{12... | collective-permute-start | bytes 3080 | tf_op jit(solution)/shard_map/ppermute | solution.py:22
  15.1 9.5 %copy-start.7 = (f32[1,64,512]{2,1,0:T(8,128)S(1)}, f32[1,64,512]{2,1,0:T(8,128)}, u32[]{:S(2)}) copy-start(f32[1,64,512]{2,1,0:T(8,128)} %param.7) | copy-start | bytes 393220
  15.1 9.5 %copy-start.11 = (f32[4,32,64]{2,1,0:T(8,128)S(1)}, f32[4,32,64]{2,1,0:T(8,128)}, u32[]{:S(2)}) copy-start(f32[4,32,64]{2,1,0:T(8,128)} %param.9) | copy-start | bytes 98308
  24.6 0.6 copy-start.17
  24.6 0.6 copy-start.19
  25.3 1.1 copy-start.4
  28.0 2.4 %copy-start.6 = (f32[1,32,1040]{2,1,0:T(8,128)}, f32[1,32,1040]{2,1,0:T(8,128)S(1)}, u32[]{:S(2)}) copy-start(f32[1,32,1040]{2,1,0:T(8,128)S(1)} %copy.17) | copy-start | bytes 399364
  32.7 5.9 %copy-start.9 = (f32[1,32,1040]{2,1,0:T(8,128)}, f32[1,32,1040]{2,1,0:T(8,128)S(1)}, u32[]{:S(2)}) copy-start(f32[1,32,1040]{2,1,0:T(8,128)S(1)} %get-tuple-element.74) | copy-start | bytes 399364
  39.6 2.0 %copy-start.14 = (f32[1,1040]{1,0:T(1,128)}, f32[1,1040]{1,0:T(1,128)S(1)}, u32[]{:S(2)}) copy-start(f32[1,1040]{1,0:T(1,128)S(1)} %squeeze.11) | copy-start | bytes 12484
  42.3 14.1 %collective-permute-start.2 = (f32[1,768]{1,0:T(1,128)}, f32[1,768]{1,0:T(1,128)}, u32[]{:S(2)}, u32[]{:S(2)}) collective-permute-start(f32[1,768]{1,0:T(1,128)} %slice.333), channel_id=1, source_target_pairs={{1,0},{2,1},{3,2},{4,3},{5,4},{6,5},{7,6},{9,8},{10,9},{11,10},{12... | collective-permute-start | bytes 9224 | tf_op jit(solution)/shard_map/ppermute | solution.py:32
  44.2 0.6 copy-start.15
  51.1 4.3 %copy-start.2 = (f32[256,128]{1,0:T(8,128)S(1)}, f32[256,128]{1,0:T(8,128)}, u32[]{:S(2)}) copy-start(f32[256,128]{1,0:T(8,128)} %get-tuple-element.75) | copy-start | bytes 393220
  51.1 4.3 %copy-start.3 = (f32[256,128]{1,0:T(8,128)S(1)}, f32[256,128]{1,0:T(8,128)}, u32[]{:S(2)}) copy-start(f32[256,128]{1,0:T(8,128)} %get-tuple-element.76) | copy-start | bytes 393220
  51.1 5.2 %copy-start.16 = (f32[1,1024]{1,0:T(1,128)S(1)}, f32[1,1024]{1,0:T(1,128)}, u32[]{:S(2)}) copy-start(f32[1,1024]{1,0:T(1,128)} %get-tuple-element.53) | copy-start | bytes 12292
  71.7 20.1 %collective-permute-start.5 = (f32[1,768]{1,0:T(1,128)S(1)}, f32[1,768]{1,0:T(1,128)S(1)}, u32[]{:S(2)}, u32[]{:S(2)}) collective-permute-start(f32[1,768]{1,0:T(1,128)S(1)} %pad.112), channel_id=1, source_target_pairs={{0,1},{1,2},{2,3},{3,4},{4,5},{5,6},{6,7},{8,9},{9,10},{10,11},{11... | collective-permute-start | bytes 9224 | tf_op jit(solution)/shard_map/ppermute | solution.py:32
  78.0 3.7 %copy-start.23 = (f32[64]{0:T(128)S(1)}, f32[64]{0:T(128)}, u32[]{:S(2)}) copy-start(f32[64]{0:T(128)} %get-tuple-element.67) | copy-start | bytes 772
  78.0 3.7 %copy-start.24 = (f32[64]{0:T(128)S(1)}, f32[64]{0:T(128)}, u32[]{:S(2)}) copy-start(f32[64]{0:T(128)} %get-tuple-element.68) | copy-start | bytes 772
  78.0 4.1 %copy-start.22 = (f32[1,4,1024]{2,1,0:T(4,128)S(1)}, f32[1,4,1024]{2,1,0:T(4,128)}, u32[]{:S(2)}) copy-start(f32[1,4,1024]{2,1,0:T(4,128)} %fusion.15) | copy-start | bytes 49156
  81.7 1.6 copy-start.1
  83.3 8.6 %copy-start.21 = (f32[1,1216]{1,0:T(1,128)S(1)}, f32[1,1216]{1,0:T(1,128)}, u32[]{:S(2)}) copy-start(f32[1,1216]{1,0:T(1,128)} %reshape.974) | copy-start | bytes 14596
  86.8 43.6 %copy-start.10 = (f32[1,32,1040]{2,1,0:T(8,128)S(1)}, f32[1,32,1040]{2,1,0:T(8,128)}, u32[]{:S(2)}) copy-start(f32[1,32,1040]{2,1,0:T(8,128)} %copy-done.9) | copy-start | bytes 399364
  86.9 6.3 %collective-permute-start.4 = (f32[1,768]{1,0:T(1,128)S(1)}, f32[1,768]{1,0:T(1,128)S(1)}, u32[]{:S(2)}, u32[]{:S(2)}) collective-permute-start(f32[1,768]{1,0:T(1,128)S(1)} %slice.347), channel_id=1, source_target_pairs={{0,1},{1,2},{2,3},{3,4},{4,5},{5,6},{6,7},{8,9},{9,10},{10,11},{11... | collective-permute-start | bytes 9224 | tf_op jit(solution)/shard_map/ppermute | solution.py:32
  122.0 5.8 %collective-permute-start.7 = (f32[1,1,8]{2,1,0:T(1,128)S(1)}, f32[1,1,8]{2,1,0:T(1,128)S(1)}, u32[]{:S(2)}, u32[]{:S(2)}) collective-permute-start(f32[1,1,8]{2,1,0:T(1,128)S(1)} %get-tuple-element.61), channel_id=1, source_target_pairs={{1,0},{2,1},{3,2},{4,3},{5,4},{6,5},{7,6},{9,8},{10,9},{11,10},{12... | collective-permute-start | bytes 104 | tf_op jit(solution)/shard_map/ppermute | solution.py:22
  123.3 5.8 %collective-permute-start.6 = (f32[1,1,8]{2,1,0:T(1,128)S(1)}, f32[1,1,8]{2,1,0:T(1,128)S(1)}, u32[]{:S(2)}, u32[]{:S(2)}) collective-permute-start(f32[1,1,8]{2,1,0:T(1,128)S(1)} %get-tuple-element.62), channel_id=1, source_target_pairs={{0,1},{1,2},{2,3},{3,4},{4,5},{5,6},{6,7},{8,9},{9,10},{10,11},{11... | collective-permute-start | bytes 104 | tf_op jit(solution)/shard_map/ppermute | solution.py:20
  129.2 3.1 %copy-start.13 = (f32[3,16,32]{2,1,0:T(8,128)S(1)}, f32[3,16,32]{2,1,0:T(8,128)}, u32[]{:S(2)}) copy-start(f32[3,16,32]{2,1,0:T(8,128)} %param.10) | copy-start | bytes 18436
  131.2 2.7 %copy-start.5 = (f32[1,64,519]{2,1,0:T(8,128)S(1)}, f32[1,64,519]{2,1,0:T(8,128)}, u32[]{:S(2)}) copy-start(f32[1,64,519]{2,1,0:T(8,128)} %copy-done.4) | copy-start | bytes 398596
  131.7 2.7 %copy-start.8 = (f32[1,64,512]{2,1,0:T(8,128)S(1)}, f32[1,64,512]{2,1,0:T(8,128)}, u32[]{:S(2)}) copy-start(f32[1,64,512]{2,1,0:T(8,128)} %param.7) | copy-start | bytes 393220
  131.7 2.7 %copy-start.18 = (f32[1,64,4]{2,1,0:T(8,128)S(1)}, f32[1,64,4]{2,1,0:T(8,128)}, u32[]{:S(2)}) copy-start(f32[1,64,4]{2,1,0:T(8,128)} %copy-done.17) | copy-start | bytes 3076
  131.7 2.7 %copy-start.20 = (f32[1,64,4]{2,1,0:T(8,128)S(1)}, f32[1,64,4]{2,1,0:T(8,128)}, u32[]{:S(2)}) copy-start(f32[1,64,4]{2,1,0:T(8,128)} %copy-done.19) | copy-start | bytes 3076
  134.0 52.6 %copy-start.12 = (f32[4,32,64]{2,1,0:T(8,128)S(1)}, f32[4,32,64]{2,1,0:T(8,128)}, u32[]{:S(2)}) copy-start(f32[4,32,64]{2,1,0:T(8,128)} %param.9) | copy-start | bytes 98308
where the time goes:
time: 190 us; the launch traced here: 188 us
  blocking collectives  63.8 us (34%)
  matrix products  37.6 us (20%)
  other arithmetic  31.8 us (17%)
  starting transfers between devices  26.4 us (14%)
  local copies, waits for them, and re-layouts  22 us (12%)
  between operations  4.65 us (2%)
  waiting for transfers between devices  1.95 us (1%)
    psum x1, blocking collectives, local(): lax.psum((local_totals[0], local_totals[1], local_totals[2], local_totals...  41.8 us
    dot_general x44, matrix products, product(): jnp.einsum(form, left, right, precision=lax.Precision.HIGHEST, preferred_...  37.6 us
    psum x1, blocking collectives, local(): squares = lax.psum(squares, 'tm')  22 us
    ppermute x4, starting transfers between devices, from_behind(): return lax.ppermute(x, axis, pairs)  13.8 us
    mul x2, other arithmetic, dft_table(): -hann_taper * jnp.sin(angles)  10.7 us
    ppermute x2, starting transfers between devices, padded_2(): lax.ppermute(tail, axis, [(i, (i + 1) % count) for i in range(ends)])  10.1 us
    reshape x5, local copies, waits for them, and re-layouts, framed(): blocks = signal.reshape(signal.shape[:-1] + (frame_count + 3, hop_size))  6.68 us
    slice x4, local copies, waits for them, and re-layouts, framed(): blocks[..., offset:offset + frame_count, :]  4.01 us
  transfers between devices with their start and end apart: 8, of which 2 were waited for; matrix products, arithmetic and copies ran while one was open for 28% of the time, Pallas kernels for 0%

commit v1 on v0

--- a/solution.py
+++ b/solution.py
@@ -254,7 +254,7 @@
     ]
     param_count = sum((member.size for member in local_totals))
     summed = lax.psum(
-        (local_totals[0], local_totals[1], local_totals[2], local_totals[3]), ("dp", "tm")
+        lax.psum((local_totals[0], local_totals[1], local_totals[2], local_totals[3]), "tm"), "dp"
     )
     squares_all = sum((jnp.sum(member * member) for member in summed))
     factor = jnp.minimum(1.0, 1.0 / jnp.sqrt(squares_all / param_count + 1e-06))

time: 190 us -> 196 us (1.032)
  blocking collectives: 63.8 us -> 69.7 us
    psum x0 -> x1, blocking collectives: none -> 11.3 us  [local(): lax.psum(lax.psum((local_totals[0], local_totals[1], local_totals[2], loc...]
    psum x1, blocking collectives: 41.8 us -> 36.4 us  [local(): lax.psum((local_totals[0], local_totals[1], local_totals[2], local_totals...]
  transfers between devices with their start and end apart: 8 -> 8, of which waited for: 2 -> 2; matrix products, arithmetic and copies ran while one was open for 28% -> 27% of each run, Pallas kernels for 0% -> 0%
where the time goes in v1:
time: 196 us; the launch traced here: 194 us
  blocking collectives  69.7 us (36%)
  matrix products  37.6 us (19%)
  other arithmetic  31.8 us (16%)
  starting transfers between devices  26.4 us (13%)
  local copies, waits for them, and re-layouts  21.8 us (11%)
  between operations  4.69 us (2%)
    dot_general x44, matrix products, product(): jnp.einsum(form, left, right, precision=lax.Precision.HIGHEST, preferred_...  37.6 us
    psum x1, blocking collectives, local(): lax.psum((local_totals[0], local_totals[1], local_totals[2], local_totals...  36.4 us
    psum x1, blocking collectives, local(): squares = lax.psum(squares, 'tm')  22 us
    ppermute x4, starting transfers between devices, from_behind(): return lax.ppermute(x, axis, pairs)  13.8 us
    psum x1, blocking collectives, local(): lax.psum(lax.psum((local_totals[0], local_totals[1], local_totals[2], loc...  11.3 us
    mul x2, other arithmetic, dft_table(): -hann_taper * jnp.sin(angles)  10.7 us
    ppermute x2, starting transfers between devices, padded_2(): lax.ppermute(tail, axis, [(i, (i + 1) % count) for i in range(ends)])  10.1 us
    reshape x5, local copies, waits for them, and re-layouts, framed(): blocks = signal.reshape(signal.shape[:-1] + (frame_count + 3, hop_size))  6.68 us
  transfers between devices with their start and end apart: 8, of which 2 were waited for; matrix products, arithmetic and copies ran while one was open for 27% of the time, Pallas kernels for 0%

profile of v1, /device:TPU:0, one launch (start us, length us, event | category | flops | bytes accessed | tf_op | source)
XLA Modules:
  0.0 194.0 jit_solution(15026343945941691035)
XLA Ops:
  0.6 1.3 slice.296
  1.9 1.3 collective-permute-start.3
  4.1 5.5 %collective-permute-start = (f32[1,64,4]{2,1,0:T(8,128)S(1)}, f32[1,64,4]{2,1,0:T(8,128)S(1)}, u32[]{:S(2)}, u32[]{:S(2)}) collective-permute-start(f32[1,64,4]{2,1,0:T(8,128)S(1)} %get-tuple-element.19), channel_id=1, source_target_pairs={{0,1},{1,2},{2,3},{3,4},{4,5},{5,6},{6,7},{8,9},{9,10},{10,11},{11... | collective-permute-start | bytes 3080 | tf_op jit(solution)/shard_map/ppermute | solution.py:20
  9.6 1.3 collective-permute-start.1
  12.3 1.6 slice_bitcast_fusion.6
  13.9 1.2 sine_multiply_fusion.1
  15.1 9.4 %sine_multiply_fusion = (f32[1024,512]{1,0:T(8,128)S(1)}, f32[1024,512]{1,0:T(8,128)}) fusion(f32[1024]{0:T(1024)S(1)} %fusion.218, f32[1024]{0:T(1024)S(1)} %multiply_subtract_fusion), kind=kLoop, calls=%fused_computation.21 | loop fusion | flops 8388608 | bytes 4202496 | tf_op jit(solution)/shard_map/jvp()/mul | solution.py:57
  25.2 1.1 compare_select_fusion
  26.5 1.2 copy.16
  28.0 1.0 fusion.69
  29.0 1.3 convolution_add_fusion.1
  30.3 1.0 fusion.5
  31.3 1.3 compare_select_fusion.9
  32.6 1.0 convolution_reduce_fusion.2
  33.6 1.0 convolution_reduce_fusion.1
  34.6 1.0 convolution_reduce_fusion
  35.5 1.0 convolution_reduce_fusion.5
  36.5 1.0 convolution_reduce_fusion.4
  37.5 1.0 convolution_reduce_fusion.6
  38.5 1.0 convolution_reduce_fusion.3
  39.5 2.0 %multiply_reduce_fusion.6 = (f32[]{:T(128)}, f32[1,1024]{1,0:T(1,128)}, f32[1,1792]{1,0:T(1,128)S(1)}) fusion(f32[1,1024]{1,0:T(1,128)} %param.8, f32[1,1040]{1,0:T(1,128)S(1)} %squeeze.11), kind=kLoop, calls=%fused_computation.340 | loop fusion | flops 4094 | bytes 16388 | tf_op jit(solution)/shard_map/reduce_sum | solution.py:220
  42.1 1.3 collective-permute-start.2
  45.3 1.3 reduce.11
  46.6 1.3 reshape.962
  47.9 1.4 reshape.970
  51.0 4.3 %fusion.15 = f32[1,4,1024]{2,1,0:T(4,128)} fusion(f32[1024,512]{1,0:T(8,128)S(1)} %get-tuple-element.81, f32[1024,512]{1,0:T(8,128)} %get-tuple-element.82, f32[1,4,256]{2,1,0:T(4,128)S(1)} %get-tuple-element.49, f32[1,4,256]{2,1,0:T(4,128)S(1)} %get-tuple-element.50, f32[1,4,256]{2,1,0:T(4,128)S(1)} %get-tuple-element.51, ...), kind=kOutput, calls=%fused_computation.33 | convolution fusion | flops 51392512 | bytes 4227072 | tf_op jit(solution)/shard_map/...nf,fk->...nk/dot_general | solution.py:36
  55.3 0.9 convolution_bitcast_fusion.10
  56.2 1.3 maximum_reduce_fusion
  57.5 1.3 reshape.959
  58.8 1.3 fusion.210
  60.1 1.4 reshape.967
  61.4 1.4 fusion.285
  63.7 1.2 convolution_bitcast_fusion.11
  65.8 0.9 fusion.20
  67.5 1.3 convolution_bitcast_fusion.9
  69.5 1.4 reshape.974
  71.6 6.3 %collective-permute-start.5 = (f32[1,768]{1,0:T(1,128)S(1)}, f32[1,768]{1,0:T(1,128)S(1)}, u32[]{:S(2)}, u32[]{:S(2)}) collective-permute-start(f32[1,768]{1,0:T(1,128)S(1)} %pad.112), channel_id=1, source_target_pairs={{0,1},{1,2},{2,3},{3,4},{4,5},{5,6},{6,7},{8,9},{9,10},{10,11},{11... | collective-permute-start | bytes 9224 | tf_op jit(solution)/shard_map/ppermute | solution.py:32
  77.9 3.7 %fusion.14 = f32[1,4,1024]{2,1,0:T(4,128)S(1)} fusion(f32[1024,512]{1,0:T(8,128)S(1)} %get-tuple-element.81, f32[1024,512]{1,0:T(8,128)} %get-tuple-element.82, f32[1,4,256]{2,1,0:T(4,128)} %get-tuple-element.53, f32[1,4,256]{2,1,0:T(4,128)} %get-tuple-element.54, f32[1,4,256]{2,1,0:T(4,128)} %get-tuple-element.55, f32[1,4,256]{2,1,0:T(4,128)} %get-tuple-element.52), kind=kOutput, calls=%fused_computation.32 | convolution fusion | flops 51392512 | bytes 4227072 | tf_op jit(solution)/shard_map/jvp(...nf,fk->...nk)/dot_general | solution.py:36
  83.2 3.5 %fusion.16 = f32[1,4,1024]{2,1,0:T(4,128)S(1)} fusion(f32[1024,512]{1,0:T(8,128)S(1)} %get-tuple-element.81, f32[1024,512]{1,0:T(8,128)S(1)} %copy-done.1, f32[1,4,512]{2,1,0:T(4,128)S(1)} %get-tuple-element.22, f32[1,4,512]{2,1,0:T(4,128)S(1)} %get-tuple-element.21), kind=kOutput, calls=%fused_computation.34 | convolution fusion | flops 51384320 | bytes 4227072 | tf_op jit(solution)/shard_map/transpose(jvp(...nf,fk->...nk))/dot_general | solution.py:36
  86.8 5.0 %collective-permute-start.4 = (f32[1,768]{1,0:T(1,128)S(1)}, f32[1,768]{1,0:T(1,128)S(1)}, u32[]{:S(2)}, u32[]{:S(2)}) collective-permute-start(f32[1,768]{1,0:T(1,128)S(1)} %slice.347), channel_id=1, source_target_pairs={{0,1},{1,2},{2,3},{3,4},{4,5},{5,6},{6,7},{8,9},{9,10},{10,11},{11... | collective-permute-start | bytes 9224 | tf_op jit(solution)/shard_map/ppermute | solution.py:32
  93.7 2.0 %pad_maximum_fusion.16 = f32[1,3]{1,0:T(1,128)S(1)} fusion(f32[1,1]{1,0:T(1,128)} %bitcast.63, f32[1,1]{1,0:T(1,128)} %bitcast.53, f32[1,1]{1,0:T(1,128)} %bitcast.43), kind=kLoop, calls=%fused_computation.344 | loop fusion | flops 6 | bytes 24 | tf_op jit(solution)/shard_map/stack | solution.py:220
  95.8 22.0 %psum.63 = f32[1,3]{1,0:T(1,128)S(1)} all-reduce(f32[1,3]{1,0:T(1,128)S(1)} %pad_maximum_fusion.16), channel_id=1, replica_groups=mesh['dp'=4,'tm'=8] {'tm'}, use_global_device_ids=true, to_apply=%region_3.4 | all-reduce | flops 3 | bytes 24 | tf_op jit(solution)/shard_map/psum | solution.py:221
  119.7 2.1 %add_bitcast_fusion.1 = f32[1,1,1024]{2,1,0:T(1,128)S(1)} fusion(f32[1,1024]{1,0:T(1,128)S(1)} %get-tuple-element.18, f32[1,1024]{1,0:T(1,128)S(1)} %get-tuple-element.16, f32[]{:T(128)} %bitcast.66, f32[]{:T(128)} %bitcast.65, f32[]{:T(128)} %bitcast.64, f32[1,1024]{1,0:T(1,128)} %param.8, f32[1,1040]{1,0:T(1,128)} %copy-done.14), kind=kLoop, calls=%fused_computation.336 | loop fusion | flops 6144 | bytes 20492 | tf_op jit(solution)/shard_map/broadcast_in_dim | solution.py:226
  121.9 1.3 collective-permute-start.7
  123.2 4.5 %collective-permute-start.6 = (f32[1,1,8]{2,1,0:T(1,128)S(1)}, f32[1,1,8]{2,1,0:T(1,128)S(1)}, u32[]{:S(2)}, u32[]{:S(2)}) collective-permute-start(f32[1,1,8]{2,1,0:T(1,128)S(1)} %get-tuple-element.66), channel_id=1, source_target_pairs={{0,1},{1,2},{2,3},{3,4},{4,5},{5,6},{6,7},{8,9},{9,10},{10,11},{11... | collective-permute-start | bytes 104 | tf_op jit(solution)/shard_map/ppermute | solution.py:20
  127.7 1.3 collective-permute-done.6
  136.7 36.4 %all-reduce.29 = (f32[4,32,64]{2,1,0:T(8,128)S(1)}, f32[3,16,32]{2,1,0:T(8,128)S(1)}, f32[32,16]{0,1:T(8,128)S(1)}, f32[7,32]{1,0:T(8,128)S(1)}) all-reduce(f32[4,32,64]{2,1,0:T(8,128)S(1)} %maximum_bitcast_fusion, f32[3,16,32]{2,1,0:T(8,128)S(1)} %maximum_bitcast_fusion.1, ...), channel_id=1, replica_groups=mesh['dp'=4,'tm'=8] {'tm'}, use_global_device_ids=true, to_apply=%region_4.5 | all-reduce | flops 10464 | bytes 83712 | tf_op jit(solution)/shard_map/psum | solution.py:257
  173.1 11.3 %all-reduce.30 = (f32[4,32,64]{2,1,0:T(8,128)S(1)}, f32[3,16,32]{2,1,0:T(8,128)S(1)}, f32[32,16]{0,1:T(8,128)S(1)}, f32[7,32]{1,0:T(8,128)S(1)}) all-reduce(f32[4,32,64]{2,1,0:T(8,128)S(1)} %get-tuple-element.5, f32[3,16,32]{2,1,0:T(8,128)S(1)} %get-tuple-element.6, ...), channel_id=1, replica_groups=mesh['dp'=4,'tm'=8] {'dp'}, use_global_device_ids=true, to_apply=%region_5.6 | all-reduce | flops 10464 | bytes 83712 | tf_op jit(solution)/shard_map/psum | solution.py:256
  (142 shorter events, 31.0 us)
Async XLA Ops:
  0.6 30.6 %copy-start = (f32[32,16]{0,1:T(8,128)S(1)}, f32[32,16]{0,1:T(8,128)}, u32[]{:S(2)}) copy-start(f32[32,16]{0,1:T(8,128)} %param.11) | copy-start | bytes 6148
  1.9 41.5 %collective-permute-start.3 = (f32[1,768]{1,0:T(1,128)}, f32[1,768]{1,0:T(1,128)}, u32[]{:S(2)}, u32[]{:S(2)}) collective-permute-start(f32[1,768]{1,0:T(1,128)} %slice.296), channel_id=1, source_target_pairs={{1,0},{2,1},{3,2},{4,3},{5,4},{6,5},{7,6},{9,8},{10,9},{11,10},{12... | collective-permute-start | bytes 9224 | tf_op jit(solution)/shard_map/ppermute | solution.py:32
  4.1 20.5 %collective-permute-start = (f32[1,64,4]{2,1,0:T(8,128)S(1)}, f32[1,64,4]{2,1,0:T(8,128)S(1)}, u32[]{:S(2)}, u32[]{:S(2)}) collective-permute-start(f32[1,64,4]{2,1,0:T(8,128)S(1)} %get-tuple-element.19), channel_id=1, source_target_pairs={{0,1},{1,2},{2,3},{3,4},{4,5},{5,6},{6,7},{8,9},{9,10},{10,11},{11... | collective-permute-start | bytes 3080 | tf_op jit(solution)/shard_map/ppermute | solution.py:20
  9.6 15.0 %collective-permute-start.1 = (f32[1,64,4]{2,1,0:T(8,128)S(1)}, f32[1,64,4]{2,1,0:T(8,128)S(1)}, u32[]{:S(2)}, u32[]{:S(2)}) collective-permute-start(f32[1,64,4]{2,1,0:T(8,128)S(1)} %get-tuple-element.20), channel_id=1, source_target_pairs={{1,0},{2,1},{3,2},{4,3},{5,4},{6,5},{7,6},{9,8},{10,9},{11,10},{12... | collective-permute-start | bytes 3080 | tf_op jit(solution)/shard_map/ppermute | solution.py:22
  15.1 9.5 %copy-start.7 = (f32[1,64,512]{2,1,0:T(8,128)S(1)}, f32[1,64,512]{2,1,0:T(8,128)}, u32[]{:S(2)}) copy-start(f32[1,64,512]{2,1,0:T(8,128)} %param.7) | copy-start | bytes 393220
  15.1 9.5 %copy-start.11 = (f32[4,32,64]{2,1,0:T(8,128)S(1)}, f32[4,32,64]{2,1,0:T(8,128)}, u32[]{:S(2)}) copy-start(f32[4,32,64]{2,1,0:T(8,128)} %param.9) | copy-start | bytes 98308
  24.6 2.0 %copy-start.17 = (f32[1,64,4]{2,1,0:T(8,128)}, f32[1,64,4]{2,1,0:T(8,128)S(1)}, u32[]{:S(2)}) copy-start(f32[1,64,4]{2,1,0:T(8,128)S(1)} %collective-permute-done) | copy-start | bytes 3076
  24.6 1.9 %copy-start.19 = (f32[1,64,4]{2,1,0:T(8,128)}, f32[1,64,4]{2,1,0:T(8,128)S(1)}, u32[]{:S(2)}) copy-start(f32[1,64,4]{2,1,0:T(8,128)S(1)} %collective-permute-done.1) | copy-start | bytes 3076
  25.2 1.1 copy-start.4
  27.9 2.4 %copy-start.6 = (f32[1,32,1040]{2,1,0:T(8,128)}, f32[1,32,1040]{2,1,0:T(8,128)S(1)}, u32[]{:S(2)}) copy-start(f32[1,32,1040]{2,1,0:T(8,128)S(1)} %copy.17) | copy-start | bytes 399364
  32.6 5.9 %copy-start.9 = (f32[1,32,1040]{2,1,0:T(8,128)}, f32[1,32,1040]{2,1,0:T(8,128)S(1)}, u32[]{:S(2)}) copy-start(f32[1,32,1040]{2,1,0:T(8,128)S(1)} %get-tuple-element.78) | copy-start | bytes 399364
  39.5 2.0 %copy-start.14 = (f32[1,1040]{1,0:T(1,128)}, f32[1,1040]{1,0:T(1,128)S(1)}, u32[]{:S(2)}) copy-start(f32[1,1040]{1,0:T(1,128)S(1)} %squeeze.11) | copy-start | bytes 12484
  42.1 14.1 %collective-permute-start.2 = (f32[1,768]{1,0:T(1,128)}, f32[1,768]{1,0:T(1,128)}, u32[]{:S(2)}, u32[]{:S(2)}) collective-permute-start(f32[1,768]{1,0:T(1,128)} %slice.333), channel_id=1, source_target_pairs={{1,0},{2,1},{3,2},{4,3},{5,4},{6,5},{7,6},{9,8},{10,9},{11,10},{12... | collective-permute-start | bytes 9224 | tf_op jit(solution)/shard_map/ppermute | solution.py:32
  44.1 0.6 copy-start.15
  51.0 4.3 %copy-start.2 = (f32[256,128]{1,0:T(8,128)S(1)}, f32[256,128]{1,0:T(8,128)}, u32[]{:S(2)}) copy-start(f32[256,128]{1,0:T(8,128)} %get-tuple-element.79) | copy-start | bytes 393220
  51.0 4.3 %copy-start.3 = (f32[256,128]{1,0:T(8,128)S(1)}, f32[256,128]{1,0:T(8,128)}, u32[]{:S(2)}) copy-start(f32[256,128]{1,0:T(8,128)} %get-tuple-element.80) | copy-start | bytes 393220
  51.0 5.2 %copy-start.16 = (f32[1,1024]{1,0:T(1,128)S(1)}, f32[1,1024]{1,0:T(1,128)}, u32[]{:S(2)}) copy-start(f32[1,1024]{1,0:T(1,128)} %get-tuple-element.57) | copy-start | bytes 12292
  71.6 20.2 %collective-permute-start.5 = (f32[1,768]{1,0:T(1,128)S(1)}, f32[1,768]{1,0:T(1,128)S(1)}, u32[]{:S(2)}, u32[]{:S(2)}) collective-permute-start(f32[1,768]{1,0:T(1,128)S(1)} %pad.112), channel_id=1, source_target_pairs={{0,1},{1,2},{2,3},{3,4},{4,5},{5,6},{6,7},{8,9},{9,10},{10,11},{11... | collective-permute-start | bytes 9224 | tf_op jit(solution)/shard_map/ppermute | solution.py:32
  77.8 3.7 %copy-start.23 = (f32[64]{0:T(128)S(1)}, f32[64]{0:T(128)}, u32[]{:S(2)}) copy-start(f32[64]{0:T(128)} %get-tuple-element.71) | copy-start | bytes 772
  77.9 3.7 %copy-start.24 = (f32[64]{0:T(128)S(1)}, f32[64]{0:T(128)}, u32[]{:S(2)}) copy-start(f32[64]{0:T(128)} %get-tuple-element.72) | copy-start | bytes 772
  77.9 4.1 %copy-start.22 = (f32[1,4,1024]{2,1,0:T(4,128)S(1)}, f32[1,4,1024]{2,1,0:T(4,128)}, u32[]{:S(2)}) copy-start(f32[1,4,1024]{2,1,0:T(4,128)} %fusion.15) | copy-start | bytes 49156
  81.6 1.6 copy-start.1
  83.2 8.6 %copy-start.21 = (f32[1,1216]{1,0:T(1,128)S(1)}, f32[1,1216]{1,0:T(1,128)}, u32[]{:S(2)}) copy-start(f32[1,1216]{1,0:T(1,128)} %reshape.974) | copy-start | bytes 14596
  86.7 43.6 %copy-start.10 = (f32[1,32,1040]{2,1,0:T(8,128)S(1)}, f32[1,32,1040]{2,1,0:T(8,128)}, u32[]{:S(2)}) copy-start(f32[1,32,1040]{2,1,0:T(8,128)} %copy-done.9) | copy-start | bytes 399364
  86.8 6.3 %collective-permute-start.4 = (f32[1,768]{1,0:T(1,128)S(1)}, f32[1,768]{1,0:T(1,128)S(1)}, u32[]{:S(2)}, u32[]{:S(2)}) collective-permute-start(f32[1,768]{1,0:T(1,128)S(1)} %slice.347), channel_id=1, source_target_pairs={{0,1},{1,2},{2,3},{3,4},{4,5},{5,6},{6,7},{8,9},{9,10},{10,11},{11... | collective-permute-start | bytes 9224 | tf_op jit(solution)/shard_map/ppermute | solution.py:32
  121.9 5.8 %collective-permute-start.7 = (f32[1,1,8]{2,1,0:T(1,128)S(1)}, f32[1,1,8]{2,1,0:T(1,128)S(1)}, u32[]{:S(2)}, u32[]{:S(2)}) collective-permute-start(f32[1,1,8]{2,1,0:T(1,128)S(1)} %get-tuple-element.65), channel_id=1, source_target_pairs={{1,0},{2,1},{3,2},{4,3},{5,4},{6,5},{7,6},{9,8},{10,9},{11,10},{12... | collective-permute-start | bytes 104 | tf_op jit(solution)/shard_map/ppermute | solution.py:22
  123.2 5.8 %collective-permute-start.6 = (f32[1,1,8]{2,1,0:T(1,128)S(1)}, f32[1,1,8]{2,1,0:T(1,128)S(1)}, u32[]{:S(2)}, u32[]{:S(2)}) collective-permute-start(f32[1,1,8]{2,1,0:T(1,128)S(1)} %get-tuple-element.66), channel_id=1, source_target_pairs={{0,1},{1,2},{2,3},{3,4},{4,5},{5,6},{6,7},{8,9},{9,10},{10,11},{11... | collective-permute-start | bytes 104 | tf_op jit(solution)/shard_map/ppermute | solution.py:20
  129.1 3.1 %copy-start.13 = (f32[3,16,32]{2,1,0:T(8,128)S(1)}, f32[3,16,32]{2,1,0:T(8,128)}, u32[]{:S(2)}) copy-start(f32[3,16,32]{2,1,0:T(8,128)} %param.10) | copy-start | bytes 18436
  131.1 2.8 %copy-start.5 = (f32[1,64,519]{2,1,0:T(8,128)S(1)}, f32[1,64,519]{2,1,0:T(8,128)}, u32[]{:S(2)}) copy-start(f32[1,64,519]{2,1,0:T(8,128)} %copy-done.4) | copy-start | bytes 398596
  131.5 2.7 %copy-start.8 = (f32[1,64,512]{2,1,0:T(8,128)S(1)}, f32[1,64,512]{2,1,0:T(8,128)}, u32[]{:S(2)}) copy-start(f32[1,64,512]{2,1,0:T(8,128)} %param.7) | copy-start | bytes 393220
  131.5 2.7 %copy-start.18 = (f32[1,64,4]{2,1,0:T(8,128)S(1)}, f32[1,64,4]{2,1,0:T(8,128)}, u32[]{:S(2)}) copy-start(f32[1,64,4]{2,1,0:T(8,128)} %copy-done.17) | copy-start | bytes 3076
  131.5 2.7 %copy-start.20 = (f32[1,64,4]{2,1,0:T(8,128)S(1)}, f32[1,64,4]{2,1,0:T(8,128)}, u32[]{:S(2)}) copy-start(f32[1,64,4]{2,1,0:T(8,128)} %copy-done.19) | copy-start | bytes 3076
  133.8 58.6 %copy-start.12 = (f32[4,32,64]{2,1,0:T(8,128)S(1)}, f32[4,32,64]{2,1,0:T(8,128)}, u32[]{:S(2)}) copy-start(f32[4,32,64]{2,1,0:T(8,128)} %param.9) | copy-start | bytes 98308
